TPU v7x, 256 devices: a whole 4x4x8 slice. The times are simulated.
256 devices in a mesh: cand: 32 (over y_lo, z, core), img: 8 (over y_hi, x).
Axes of the slice: x: 4, y: 4 (y_hi: 2, y_lo: 2; y = y_hi * 2 + y_lo), z: 8, core: 2. Of those that a mesh axis runs over, the one named last changes fastest.
Arguments:
- first_maps: float32 [8, 256, 344], P('img', 'cand'), may hold values from -6 to 6
- layer_of: int32 [32], P('cand'), may hold values from 0 to 1, as said below
- expand_half: int32 [32], P('cand'), may hold values from 1 to 2
- radius: int32 [32], P('cand'), may hold values from 1 to 2
- teach_up: bfloat16 [2, 344, 2064], replicated, may hold values from -0.3125 to 0.3125
- teach_dw: float32 [2, 25, 2064], replicated, may hold values from -1.25 to 1.25
- teach_down: bfloat16 [2, 344, 2064], replicated, may hold values from -0.125 to 0.125
- cand_up: bfloat16 [32, 344, 2064], P('cand'), may hold values from -0.3125 to 0.3125
- cand_dw: float32 [32, 25, 2064], P('cand'), may hold values from -1.25 to 1.25
- cand_down: bfloat16 [32, 344, 2064], P('cand'), may hold values from -0.125 to 0.125
Outputs:
- grad_up: float32 [32, 344, 2064], P('cand', None, 'img')
- grad_dw: float32 [32, 25, 2064], P('cand', None, 'img')
- grad_down: float32 [32, 344, 2064], P('cand', None, 'img')
Inputs may be any that keep to these rules, and one draw needn't show every extreme that they name: `layer_of`: both layers have at least one candidate.
All inputs are finite; a program needn't handle non-finite values.
Results may differ from a plain program's by a relative error of at most 0.014.
Values may be sent and summed in bfloat16 or wider, within the bound.
A program may use at most 192 MiB of HBM per device.

v0:
```python
import jax
import jax.numpy as jnp
from jax import lax
from jax.sharding import PartitionSpec as P

HID = 2064
H = 16


def spread(block, axis, source):
    block = jnp.where(lax.axis_index(axis) == source, block, jnp.zeros_like(block))
    return lax.psum(block, axis)


def apply_block(map_in, w_up, w_dw, w_down, unit_mask, tap_mask):
    batch_size = map_in.shape[0]
    flat_rows = map_in.reshape(-1, map_in.shape[2]).astype(jnp.bfloat16)
    preact = jnp.dot(flat_rows, w_up, preferred_element_type=jnp.float32)
    expanded = jax.nn.silu(preact) * unit_mask
    grid_maps = expanded.reshape(batch_size, H, H, expanded.shape[1])
    padded = jnp.pad(grid_maps, ((0, 0), (2, 2), (2, 2), (0, 0)))
    tap_weights = w_dw * tap_mask[:, None]
    accumulated = jnp.zeros_like(grid_maps)
    for tap_row in range(5):
        for tap_col in range(5):
            accumulated = (
                accumulated
                + tap_weights[tap_row * 5 + tap_col]
                * padded[:, tap_row : tap_row + H, tap_col : tap_col + H, :]
            )
    activated = jax.nn.silu(accumulated).reshape(-1, grid_maps.shape[3]).astype(jnp.bfloat16)
    branch = lax.dot_general(
        activated, w_down, (((1,), (1,)), ((), ())), preferred_element_type=jnp.float32
    )
    return map_in + branch.reshape(map_in.shape)


def make_masks(half_count, kernel_radius):
    unit_index = lax.broadcasted_iota(jnp.int32, (HID,), 0)
    unit_mask = (unit_index < half_count * (HID // 2)).astype(jnp.float32)
    tap_index = lax.broadcasted_iota(jnp.int32, (25,), 0)
    shift_row = tap_index // 5 - 2
    shift_col = tap_index % 5 - 2
    tap_mask = (jnp.maximum(jnp.abs(shift_row), jnp.abs(shift_col)) <= kernel_radius).astype(
        jnp.float32
    )
    return (unit_mask, tap_mask)


def candidate_grads(inputs, target, w_up, w_dw, w_down, unit_mask, tap_mask, images):

    def squared_loss(up_wide, depth_weights, down_wide):
        result = apply_block(
            inputs,
            up_wide.astype(jnp.bfloat16),
            depth_weights,
            down_wide.astype(jnp.bfloat16),
            unit_mask,
            tap_mask,
        )
        error_map = result - target
        return 0.5 * jnp.sum(error_map * error_map) / images

    return jax.grad(squared_loss, argnums=(0, 1, 2))(
        w_up.astype(jnp.float32), w_dw, w_down.astype(jnp.float32)
    )


def body(
    first_maps,
    layer_of,
    expand_half,
    radius,
    teach_up,
    teach_dw,
    teach_down,
    cand_up,
    cand_dw,
    cand_down,
):
    cand_index = lax.axis_index("cand")
    layer_here = layer_of[0]
    maps_zero = lax.all_gather(first_maps, "cand", axis=1, tiled=True)
    full_units = jnp.ones((HID,), jnp.float32)
    all_taps = jnp.ones((25,), jnp.float32)

    def teacher(map_in, depth_level):
        return apply_block(
            map_in,
            teach_up[depth_level],
            teach_dw[depth_level],
            teach_down[depth_level],
            full_units,
            all_taps,
        )

    beyond = jnp.int32(lax.axis_size("cand"))
    owner_ranks = lax.pmin(
        (
            jnp.where(layer_here == 0, cand_index, beyond),
            jnp.where(layer_here == 1, cand_index, beyond),
        ),
        "cand",
    )

    def announce(map_in, depth_level, owner_rank):
        produced = lax.cond(
            cand_index == owner_rank,
            lambda: teacher(map_in, depth_level),
            lambda: jnp.zeros_like(map_in),
        )
        return spread(produced.astype(jnp.bfloat16), "cand", owner_rank).astype(produced.dtype)

    maps_one = announce(maps_zero, 0, owner_ranks[0])
    maps_two = announce(maps_one, 1, owner_ranks[1])
    inputs = jnp.where(layer_here == 0, maps_zero, maps_one)
    target = jnp.where(layer_here == 0, maps_one, maps_two)
    unit_mask, tap_mask = make_masks(expand_half[0], radius[0])
    images = maps_zero.shape[0] * lax.axis_size("img")
    gradients = candidate_grads(
        inputs, target, cand_up[0], cand_dw[0], cand_down[0], unit_mask, tap_mask, images
    )
    summed = (
        lax.psum_scatter(
            gradients[0][None].astype(jnp.bfloat16), "img", scatter_dimension=2, tiled=True
        ).astype(jnp.float32),
        lax.psum_scatter(
            gradients[1][None].astype(jnp.bfloat16), "img", scatter_dimension=2, tiled=True
        ).astype(jnp.float32),
        lax.psum_scatter(
            gradients[2][None].astype(jnp.bfloat16), "img", scatter_dimension=2, tiled=True
        ).astype(jnp.float32),
    )
    return (summed[0], summed[1], summed[2])


def solution(mesh):
    placed = (
        P("img", "cand", None),
        P("cand"),
        P("cand"),
        P("cand"),
        P(),
        P(),
        P(),
        P("cand", None, None),
        P("cand", None, None),
        P("cand", None, None),
    )
    return jax.shard_map(
        body,
        mesh=mesh,
        in_specs=placed,
        out_specs=(P("cand", None, "img"), P("cand", None, "img"), P("cand", None, "img")),
        check_vma=False,
    )
```

profile of v0, /device:TPU:32, one launch (start us, length us, event | category | flops | bytes accessed | tf_op | source)
XLA Modules:
  0.0 738.2 jit_solution(10471688653235527905)
XLA Ops:
  8.0 19.1 %all-reduce.56 = (s32[]{:T(128)}, s32[]{:T(128)}) all-reduce(s32[]{:T(128)S(6)} %select_n.53, s32[]{:T(128)S(6)} %select_n.59), channel_id=1, replica_groups=mesh['cand'=32,'img'=8] {'cand'}, use_global_device_ids=true, to_apply=%region_0.1 | all-reduce | flops 2 | bytes 16 | tf_op jit(solution)/shard_map/pmin | solution.py:98
  27.7 0.7 copy.30
  28.5 32.4 %all_gather.3 = f32[1,256,344]{2,0,1:T(1,128)S(1)} all-gather(f32[1,8,344]{2,0,1:T(1,128)S(1)} %copy.30), channel_id=1, replica_groups=mesh['cand'=32,'img'=8] {'cand'}, dimensions={1}, use_global_device_ids=true | all-gather | bytes 363264 | tf_op jit(solution)/shard_map/all_gather | solution.py:83
  60.9 0.7 broadcast_select_fusion.1
  63.1 0.7 slice_reduce_fusion.73
  64.8 1.0 slice_reduce_fusion.74
  65.9 238.3 %all-reduce.62.cloned.1.call-done = bf16[1,256,344]{1,2,0:T(8,128)(2,1)} async-done(((bf16[1,256,344]{1,2,0:T(8,128)(2,1)}), bf16[1,256,344]{1,2,0:T(8,128)(2,1)}) %all-reduce.62.cloned.1.call-update) | async-done | bytes 176144 | tf_op jit(solution)/shard_map/psum | solution.py:12
  304.2 1.0 fusion.181
  305.2 3.1 multiply_multiply_fusion
  308.3 2.0 copy.34
  310.5 0.7 broadcast_select_fusion
  311.4 9.7 %multiply_convert_fusion.2 = (bf16[1,16,16,2064]{3,2,1,0:T(8,128)(2,1)S(1)}, f32[1,16,16,2064]{3,2,1,0:T(8,128)}) fusion(f32[2064]{0:T(1024)S(1)} %get-tuple-element.143, f32[2064]{0:T(1024)S(1)} %get-tuple-element.144, f32[2064]{0:T(1024)S(1)} %get-tuple-element.145, f32[2064]{0:T(1024)S(1)} %get-tuple-element.146, f32[2064]{0:T(1024)S(1)} %get-tuple-element.147, ...), kind=kLoop, calls=%fused_computation.286 | loop fusion | flops 28532736 | bytes 5490240 | tf_op jit(solution)/shard_map/jvp()/convert_element_type | solution.py:31
  321.2 230.1 %all-reduce.64.cloned.1.call-done = bf16[1,256,344]{1,2,0:T(8,128)(2,1)} async-done(((bf16[1,256,344]{1,2,0:T(8,128)(2,1)}), bf16[1,256,344]{1,2,0:T(8,128)(2,1)}) %all-reduce.64.cloned.1.call-update) | async-done | bytes 176144 | tf_op jit(solution)/shard_map/psum | solution.py:12
  551.3 2.3 fusion.165
  553.6 2.2 fusion.134
  555.8 3.0 copy.36
  558.8 4.5 multiply_reduce_fusion.23
  563.6 6.6 multiply_reduce_fusion.24
  570.4 12.9 %broadcast_multiply_fusion.24 = (f32[1,16,16,2064]{3,2,1,0:T(8,128)}, f32[1,16,16,2064]{3,2,1,0:T(8,128)}, f32[1,16,16,2064]{3,2,1,0:T(8,128)}, f32[1,16,16,2064...) fusion(f32[1,16,16,2064]{3,2,1,0:T(8,128)S(1)} %get-tuple-eleme, ...), kind=kLoop, calls=%fused_computation.331 | loop fusion | flops 9510912 | bytes 40305792 | tf_op jit(solution)/shard_map/transpose(jvp())/mul | solution.py:28
  583.4 5.5 broadcast_multiply_fusion
  588.9 1.8 fusion.136
  591.5 0.8 convert_element_type.135
  592.3 16.1 %pad_add_fusion = f32[1,20,20,2064]{3,2,1,0:T(8,128)S(1)} fusion(f32[1,16,16,2064]{3,2,1,0:T(8,128)} %get-tuple-element.183, f32[1,16,16,2064]{3,2,1,0:T(8,128)} %get-tuple-element.184, f32[1,16,16,2064]{3,2,1,0:T(8,128)} %get-tuple-element.185, f32[1,16,16,2064]{3,2,1,0:T(8,128)} %get-tuple-element.186, f32[1,16,16,2064]{3,2,1,0:T(8,128)} %get-tuple-element.187, ...), kind=kLoop, calls=%fused_computation.244 | loop fusion | flops 14860800 | bytes 43459584 | tf_op jit(solution)/shard_map/transpose(jvp())/add_any | solution.py:29
  608.4 7.1 pad_add_fusion.1
  615.6 2.0 copy.37
  617.6 3.9 fusion.135
  621.5 0.6 copy-done.50
  623.4 103.0 %all-reduce.66.cloned.1.call-done = (bf16[1,344,2064]{2,1,0:T(8,128)(2,1)}, bf16[1,25,2064]{2,0,1:T(2,128)(2,1)}, bf16[1,344,2064]{2,1,0:T(8,128)(2,1)}) async-done(((bf16[1,344,2064]{2,1,0:T(8,128)(2,1)}, bf16[1,25,2064]{2,0,1:T(2,128)(2,1)}, bf16[1,344,2064]{2,1,0:T(8,128)(2,1)}), (bf16[1,344,2064]{2,1,0:T(8,128)(2,1)}, bf16[1,25,2064]{2,0,1:T(2,128)(2,1)}, ...) | async-done | bytes 2943280
  726.4 1.3 dynamic-slice_convert_fusion
  727.7 1.2 copy.38
  728.9 1.2 copy.39
  730.1 1.6 dynamic-slice_convert_fusion.2
  (138 shorter events, 2.3 us)
Async XLA Ops:
  7.2 298.0 %copy-start = (bf16[1,344,2064]{2,1,0:T(8,128)(2,1)S(1)}, bf16[1,344,2064]{2,1,0:T(8,128)(2,1)}, u32[]{:S(2)}) copy-start(bf16[1,344,2064]{2,1,0:T(8,128)(2,1)} %param.21) | copy-start | bytes 4260100
  7.2 297.0 %all-reduce.62.cloned.1.call-start = ((), (), s32[]{:S(2)}) async-start(), calls=%async_computation | async-start | bytes 352256 | tf_op jit(solution)/shard_map/psum | solution.py:12
  61.6 489.7 %all-reduce.64.cloned.1.call-start = ((), (), s32[]{:S(2)}) async-start(), calls=%async_computation.1 | async-start | bytes 352256 | tf_op jit(solution)/shard_map/psum | solution.py:12
  63.8 244.4 %copy-start.44 = (f32[2064]{0:T(1024)}, f32[2064]{0:T(1024)S(1)}, u32[]{:S(2)}) copy-start(f32[2064]{0:T(1024)S(1)} %fusion.173) | copy-start | bytes 24772
  64.2 241.0 %copy-start.4 = (f32[1,256,344]{1,2,0:T(8,128)}, f32[1,256,344]{1,2,0:T(8,128)S(1)}, u32[]{:S(2)}) copy-start(f32[1,256,344]{1,2,0:T(8,128)S(1)} %copy.33) | copy-start | bytes 1056772
  65.8 245.5 %copy-start.8 = (f32[2064]{0:T(1024)}, f32[2064]{0:T(1024)S(1)}, u32[]{:S(2)}) copy-start(f32[2064]{0:T(1024)S(1)} %get-tuple-element.147) | copy-start | bytes 24772
  65.8 245.5 %copy-start.10 = (f32[2064]{0:T(1024)}, f32[2064]{0:T(1024)S(1)}, u32[]{:S(2)}) copy-start(f32[2064]{0:T(1024)S(1)} %get-tuple-element.148) | copy-start | bytes 24772
  65.8 245.5 %copy-start.12 = (f32[2064]{0:T(1024)}, f32[2064]{0:T(1024)S(1)}, u32[]{:S(2)}) copy-start(f32[2064]{0:T(1024)S(1)} %get-tuple-element.149) | copy-start | bytes 24772
  65.8 245.5 %copy-start.14 = (f32[2064]{0:T(1024)}, f32[2064]{0:T(1024)S(1)}, u32[]{:S(2)}) copy-start(f32[2064]{0:T(1024)S(1)} %get-tuple-element.150) | copy-start | bytes 24772
  65.8 245.5 %copy-start.16 = (f32[2064]{0:T(1024)}, f32[2064]{0:T(1024)S(1)}, u32[]{:S(2)}) copy-start(f32[2064]{0:T(1024)S(1)} %get-tuple-element.143) | copy-start | bytes 24772
  65.8 245.5 %copy-start.18 = (f32[2064]{0:T(1024)}, f32[2064]{0:T(1024)S(1)}, u32[]{:S(2)}) copy-start(f32[2064]{0:T(1024)S(1)} %get-tuple-element.151) | copy-start | bytes 24772
  65.9 245.5 %copy-start.20 = (f32[2064]{0:T(1024)}, f32[2064]{0:T(1024)S(1)}, u32[]{:S(2)}) copy-start(f32[2064]{0:T(1024)S(1)} %get-tuple-element.152) | copy-start | bytes 24772
  65.9 245.5 %copy-start.22 = (f32[2064]{0:T(1024)}, f32[2064]{0:T(1024)S(1)}, u32[]{:S(2)}) copy-start(f32[2064]{0:T(1024)S(1)} %get-tuple-element.153) | copy-start | bytes 24772
  65.9 245.5 %copy-start.24 = (f32[2064]{0:T(1024)}, f32[2064]{0:T(1024)S(1)}, u32[]{:S(2)}) copy-start(f32[2064]{0:T(1024)S(1)} %get-tuple-element.154) | copy-start | bytes 24772
  65.9 245.5 %copy-start.26 = (f32[2064]{0:T(1024)}, f32[2064]{0:T(1024)S(1)}, u32[]{:S(2)}) copy-start(f32[2064]{0:T(1024)S(1)} %get-tuple-element.155) | copy-start | bytes 24772
  65.9 245.5 %copy-start.28 = (f32[2064]{0:T(1024)}, f32[2064]{0:T(1024)S(1)}, u32[]{:S(2)}) copy-start(f32[2064]{0:T(1024)S(1)} %get-tuple-element.156) | copy-start | bytes 24772
  65.9 245.5 %copy-start.30 = (f32[2064]{0:T(1024)}, f32[2064]{0:T(1024)S(1)}, u32[]{:S(2)}) copy-start(f32[2064]{0:T(1024)S(1)} %get-tuple-element.157) | copy-start | bytes 24772
  65.9 245.5 %copy-start.32 = (f32[2064]{0:T(1024)}, f32[2064]{0:T(1024)S(1)}, u32[]{:S(2)}) copy-start(f32[2064]{0:T(1024)S(1)} %get-tuple-element.158) | copy-start | bytes 24772
  65.9 245.5 %copy-start.34 = (f32[2064]{0:T(1024)}, f32[2064]{0:T(1024)S(1)}, u32[]{:S(2)}) copy-start(f32[2064]{0:T(1024)S(1)} %get-tuple-element.159) | copy-start | bytes 24772
  311.2 415.1 %all-reduce.66.cloned.1.call-start = ((), (), s32[]{:S(2)}) async-start(), calls=%async_computation.2 | async-start | bytes 6423552
  563.4 6.8 copy-start.17
  563.4 6.8 copy-start.19
  563.4 6.8 copy-start.21
  563.4 6.8 copy-start.23
  563.4 6.8 copy-start.25
  563.4 6.8 copy-start.27
  563.4 6.8 copy-start.29
  570.4 13.0 %copy-start.9 = (f32[2064]{0:T(1024)S(1)}, f32[2064]{0:T(1024)}, u32[]{:S(2)}) copy-start(f32[2064]{0:T(1024)} %copy-done.8) | copy-start | bytes 24772
  570.4 13.0 %copy-start.11 = (f32[2064]{0:T(1024)S(1)}, f32[2064]{0:T(1024)}, u32[]{:S(2)}) copy-start(f32[2064]{0:T(1024)} %copy-done.10) | copy-start | bytes 24772
  570.4 13.0 %copy-start.13 = (f32[2064]{0:T(1024)S(1)}, f32[2064]{0:T(1024)}, u32[]{:S(2)}) copy-start(f32[2064]{0:T(1024)} %copy-done.12) | copy-start | bytes 24772
  570.4 13.0 %copy-start.15 = (f32[2064]{0:T(1024)S(1)}, f32[2064]{0:T(1024)}, u32[]{:S(2)}) copy-start(f32[2064]{0:T(1024)} %copy-done.14) | copy-start | bytes 24772
  621.5 110.2 %copy-start.1 = (bf16[1,344,2064]{2,1,0:T(8,128)(2,1)S(1)}, bf16[1,344,2064]{2,1,0:T(8,128)(2,1)}, u32[]{:S(2)}) copy-start(bf16[1,344,2064]{2,1,0:T(8,128)(2,1)} %param.21) | copy-start | bytes 4260100
  (20 other events, 92.3 us)
Sparse Core Ops, SparseCore 0:
  61.7 242.4 all-reduce.61
  311.4 239.8 all-reduce.63
  621.6 104.7 all-reduce.65
where the time goes:
time: 739 us; the launch traced here: 738 us
  waiting for transfers between devices  571 us (77%)
  other arithmetic  68.4 us (9%)
  blocking collectives  51.5 us (7%)
  between operations  18.6 us (3%)
  local copies, waits for them, and re-layouts  14.7 us (2%)
  matrix products  13.2 us (2%)
    psum x2, waiting for transfers between devices, spread(): return lax.psum(block, axis)  468 us
    unnamed x4, waiting for transfers between devices  103 us
    all_gather x1, blocking collectives, body(): maps_zero = lax.all_gather(first_maps, 'cand', axis=1, tiled=True)  32.4 us
    add_any x2, other arithmetic, apply_block(): padded[:, tap_row:tap_row + H, tap_col:tap_col + H, :]  23.3 us
    pmin x1, blocking collectives, body(): lax.pmin((jnp.where(layer_here == 0, cand_index, beyond), jnp.where(layer...  19.1 us
    mul x2, other arithmetic, apply_block(): tap_weights[tap_row * 5 + tap_col]  18.5 us
  transfers between devices with their start and end apart: 3, of which 3 were waited for; matrix products, arithmetic and copies ran while one was open for 2% of the time, Pallas kernels for 0%

commit v1 on v0

--- a/solution.py
+++ b/solution.py
@@ -9,7 +9,7 @@
 
 def spread(block, axis, source):
     block = jnp.where(lax.axis_index(axis) == source, block, jnp.zeros_like(block))
-    return lax.psum(block, axis)
+    return jnp.sum(lax.all_gather(block, axis), axis=0)
 
 
 def apply_block(map_in, w_up, w_dw, w_down, unit_mask, tap_mask):

time: 739 us -> 463 us (0.63)
  waiting for transfers between devices: 571 us -> 286 us
  other arithmetic: 68.4 us -> 76.7 us
    psum x2 -> x0, waiting for transfers between devices: 468 us -> none  [spread(): return lax.psum(block, axis)]
    all_gather x0 -> x2, waiting for transfers between devices: none -> 182 us  [spread(): return jnp.sum(lax.all_gather(block, axis), axis=0)]
    reduce_sum x0 -> x2, other arithmetic: none -> 7.73 us  [spread(): return jnp.sum(lax.all_gather(block, axis), axis=0)]
  transfers between devices with their start and end apart: 3 -> 3, of which waited for: 3 -> 3; matrix products, arithmetic and copies ran while one was open for 2% -> 4% of each run, Pallas kernels for 0% -> 0%
where the time goes in v1:
time: 463 us; the launch traced here: 462 us
  waiting for transfers between devices  286 us (62%)
  other arithmetic  76.7 us (17%)
  blocking collectives  51.5 us (11%)
  between operations  18.5 us (4%)
  local copies, waits for them, and re-layouts  15.3 us (3%)
  matrix products  13.1 us (3%)
    all_gather x2, waiting for transfers between devices, spread(): return jnp.sum(lax.all_gather(block, axis), axis=0)  182 us
    unnamed x4, waiting for transfers between devices  105 us
    all_gather x1, blocking collectives, body(): maps_zero = lax.all_gather(first_maps, 'cand', axis=1, tiled=True)  32.4 us
    add_any x2, other arithmetic, apply_block(): padded[:, tap_row:tap_row + H, tap_col:tap_col + H, :]  23.1 us
    pmin x1, blocking collectives, body(): lax.pmin((jnp.where(layer_here == 0, cand_index, beyond), jnp.where(layer...  19.1 us
    mul x2, other arithmetic, apply_block(): tap_weights[tap_row * 5 + tap_col]  18.5 us
    reduce_sum x2, other arithmetic, apply_block(): tap_weights[tap_row * 5 + tap_col]  11.1 us
    convert_element_type x1, other arithmetic, apply_block(): jax.nn.silu(accumulated).reshape(-1, grid_maps.shape[3])  9.79 us
  transfers between devices with their start and end apart: 3, of which 3 were waited for; matrix products, arithmetic and copies ran while one was open for 4% of the time, Pallas kernels for 0%

profile of v1, /device:TPU:32, one launch (start us, length us, event | category | flops | bytes accessed | tf_op | source)
XLA Modules:
  0.0 462.1 jit_solution(7572799036806881364)
XLA Ops:
  8.0 19.1 %all-reduce.56 = (s32[]{:T(128)}, s32[]{:T(128)}) all-reduce(s32[]{:T(128)S(6)} %select_n.61, s32[]{:T(128)S(6)} %select_n.67), channel_id=1, replica_groups=mesh['cand'=32,'img'=8] {'cand'}, use_global_device_ids=true, to_apply=%region_0.1 | all-reduce | flops 2 | bytes 16 | tf_op jit(solution)/shard_map/pmin | solution.py:98
  27.7 0.7 copy.30
  28.5 32.4 %all_gather.15 = f32[1,256,344]{2,0,1:T(1,128)S(1)} all-gather(f32[1,8,344]{2,0,1:T(1,128)S(1)} %copy.30), channel_id=1, replica_groups=mesh['cand'=32,'img'=8] {'cand'}, dimensions={1}, use_global_device_ids=true | all-gather | bytes 363264 | tf_op jit(solution)/shard_map/all_gather | solution.py:83
  62.3 100.8 %all-gather.5.cloned.1.call-done = bf16[32,256,344]{1,2,0:T(8,128)(2,1)} async-done(((bf16[1,256,344]{1,2,0:T(8,128)(2,1)}), bf16[32,256,344]{1,2,0:T(8,128)(2,1)}) %all-gather.5.cloned.1.call-update) | async-done | bytes 5636112 | tf_op jit(solution)/shard_map/all_gather | solution.py:12
  163.1 3.5 reduce.29
  166.7 0.8 bitcast_convert_fusion
  170.4 1.0 bitcast_multiply_fusion
  171.4 0.7 slice_reduce_fusion.73
  172.1 1.0 slice_reduce_fusion.74
  173.2 3.1 multiply_multiply_fusion
  176.3 2.0 copy.34
  178.3 9.8 %multiply_convert_fusion.2 = (bf16[1,16,16,2064]{3,2,1,0:T(8,128)(2,1)S(1)}, f32[1,16,16,2064]{3,2,1,0:T(8,128)}) fusion(f32[2064]{0:T(1024)} %get-tuple-element.143, f32[2064]{0:T(1024)S(1)} %get-tuple-element.144, f32[2064]{0:T(1024)S(1)} %get-tuple-element.145, f32[2064]{0:T(1024)S(1)} %get-tuple-element.146, f32[2064]{0:T(1024)} %get-tuple-element.147, ...), kind=kLoop, calls=%fused_computation.286 | loop fusion | flops 28532736 | bytes 5490240 | tf_op jit(solution)/shard_map/jvp()/convert_element_type | solution.py:31
  188.1 80.9 %all-gather.7.cloned.1.call-done = bf16[32,256,344]{1,2,0:T(8,128)(2,1)} async-done(((bf16[1,256,344]{1,2,0:T(8,128)(2,1)}), bf16[32,256,344]{1,2,0:T(8,128)(2,1)}) %all-gather.7.cloned.1.call-update) | async-done | bytes 5636112 | tf_op jit(solution)/shard_map/all_gather | solution.py:12
  269.0 4.2 reduce.30
  273.2 2.2 fusion.165
  276.1 2.2 fusion.134
  278.3 3.0 copy.36
  281.3 4.5 multiply_reduce_fusion.23
  286.0 6.6 %multiply_reduce_fusion.24 = (f32[2064]{0:T(1024)S(1)}, f32[2064]{0:T(1024)S(1)}, f32[2064]{0:T(1024)S(1)}, f32[2064]{0:T(1024)S(1)}, f32[2064]{0:T(1024)S(1)}, ...) fusion(f32[1,16,16,2064]{3,2,1,0:T(8,128)S(1)} %get-tuple-eleme, ...), kind=kLoop, calls=%fused_computation.285 | loop fusion | flops 18984672 | bytes 4375680 | tf_op jit(solution)/shard_map/transpose(jvp())/reduce_sum | solution.py:28
  292.8 12.9 %broadcast_multiply_fusion.24 = (f32[1,16,16,2064]{3,2,1,0:T(8,128)}, f32[1,16,16,2064]{3,2,1,0:T(8,128)}, f32[1,16,16,2064]{3,2,1,0:T(8,128)}, f32[1,16,16,2064...) fusion(f32[1,16,16,2064]{3,2,1,0:T(8,128)S(1)} %get-tuple-eleme, ...), kind=kLoop, calls=%fused_computation.331 | loop fusion | flops 9510912 | bytes 40305792 | tf_op jit(solution)/shard_map/transpose(jvp())/mul | solution.py:28
  305.8 5.5 %broadcast_multiply_fusion = (f32[1,16,16,2064]{3,2,1,0:T(8,128)}, f32[1,16,16,2064]{3,2,1,0:T(8,128)}, f32[1,16,16,2064]{3,2,1,0:T(8,128)}, f32[1,16,16,2064]{3...) fusion(f32[1,16,16,2064]{3,2,1,0:T(8,128)S(1)} %get-tuple-element.173, ...), kind=kLoop, calls=%fused_computation.307 | loop fusion | flops 3698688 | bytes 16966080 | tf_op jit(solution)/shard_map/transpose(jvp())/mul | solution.py:28
  311.4 1.8 fusion.136
  313.9 0.8 convert_element_type.167
  314.7 15.9 %pad_add_fusion = f32[1,20,20,2064]{3,2,1,0:T(8,128)S(1)} fusion(f32[1,16,16,2064]{3,2,1,0:T(8,128)} %get-tuple-element.183, f32[1,16,16,2064]{3,2,1,0:T(8,128)} %get-tuple-element.184, f32[1,16,16,2064]{3,2,1,0:T(8,128)} %get-tuple-element.185, f32[1,16,16,2064]{3,2,1,0:T(8,128)} %get-tuple-element.186, f32[1,16,16,2064]{3,2,1,0:T(8,128)} %get-tuple-element.187, ...), kind=kLoop, calls=%fused_computation.244 | loop fusion | flops 14860800 | bytes 43459584 | tf_op jit(solution)/shard_map/transpose(jvp())/add_any | solution.py:29
  330.7 7.1 %pad_add_fusion.1 = f32[1,16,16,2064]{3,2,1,0:T(8,128)} fusion(f32[1,16,16,2064]{3,2,1,0:T(8,128)} %get-tuple-element.177, f32[1,16,16,2064]{3,2,1,0:T(8,128)} %get-tuple-element.178, f32[1,16,16,2064]{3,2,1,0:T(8,128)} %get-tuple-element.179, f32[1,16,16,2064]{3,2,1,0:T(8,128)} %get-tuple-element.180, f32[1,16,16,2064]{3,2,1,0:T(8,128)} %get-tuple-element.181, ...), kind=kLoop, calls=%fused_computation.255 | loop fusion | flops 3170304 | bytes 16908288 | tf_op jit(solution)/shard_map/transpose(jvp())/add_any | solution.py:29
  337.8 2.0 copy.37
  339.8 3.9 fusion.135
  345.6 104.7 %all-reduce.60.cloned.1.call-done = (bf16[1,344,2064]{2,1,0:T(8,128)(2,1)}, bf16[1,25,2064]{2,0,1:T(2,128)(2,1)}, bf16[1,344,2064]{2,1,0:T(8,128)(2,1)}) async-done(((bf16[1,344,2064]{2,1,0:T(8,128)(2,1)}, bf16[1,25,2064]{2,0,1:T(2,128)(2,1)}, bf16[1,344,2064]{2,1,0:T(8,128)(2,1)}), (bf16[1,344,2064]{2,1,0:T(8,128)(2,1)}, bf16[1,25,2064]{2,0,1:T(2,128)(2,1)}, ...) | async-done | bytes 2943280
  450.3 1.3 dynamic-slice_convert_fusion
  451.6 1.2 copy.38
  452.8 1.2 copy.39
  454.0 1.6 dynamic-slice_convert_fusion.2
  (115 shorter events, 5.1 us)
Async XLA Ops:
  7.2 166.0 %copy-start = (bf16[1,344,2064]{2,1,0:T(8,128)(2,1)S(1)}, bf16[1,344,2064]{2,1,0:T(8,128)(2,1)}, u32[]{:S(2)}) copy-start(bf16[1,344,2064]{2,1,0:T(8,128)(2,1)} %param.21) | copy-start | bytes 4260100
  7.2 156.0 %all-gather.5.cloned.1.call-start = ((), (), s32[]{:S(2)}) async-start(), calls=%async_computation | async-start | bytes 5812224 | tf_op jit(solution)/shard_map/all_gather | solution.py:12
  61.6 207.3 %all-gather.7.cloned.1.call-start = ((), (), s32[]{:S(2)}) async-start(), calls=%async_computation.1 | async-start | bytes 5812224 | tf_op jit(solution)/shard_map/all_gather | solution.py:12
  62.3 105.1 %copy-start.2 = (f32[2,25,2064]{2,0,1:T(2,128)S(1)}, f32[2,25,2064]{2,0,1:T(2,128)}, u32[]{:S(2)}) copy-start(f32[2,25,2064]{2,0,1:T(2,128)} %param.19) | copy-start | bytes 1238404
  168.3 282.0 %all-reduce.60.cloned.1.call-start = ((), (), s32[]{:S(2)}) async-start(), calls=%async_computation.2 | async-start | bytes 6423552
  169.0 7.3 %copy-start.4 = (f32[1,256,344]{1,2,0:T(8,128)}, f32[1,256,344]{1,2,0:T(8,128)S(1)}, u32[]{:S(2)}) copy-start(f32[1,256,344]{1,2,0:T(8,128)S(1)} %copy.33) | copy-start | bytes 1056772
  170.3 6.0 %copy-start.34 = (f32[25]{0:T(128)}, f32[25]{0:T(128)S(1)}, u32[]{:S(2)}) copy-start(f32[25]{0:T(128)S(1)} %compare_convert_fusion) | copy-start | bytes 304
  170.3 6.0 %copy-start.32 = (f32[2064]{0:T(1024)}, f32[2064]{0:T(1024)S(1)}, u32[]{:S(2)}) copy-start(f32[2064]{0:T(1024)S(1)} %fusion.172) | copy-start | bytes 24772
  285.8 6.8 %copy-start.14 = (f32[2064]{0:T(1024)S(1)}, f32[2064]{0:T(1024)}, u32[]{:S(2)}) copy-start(f32[2064]{0:T(1024)} %get-tuple-element.143) | copy-start | bytes 24772
  285.8 6.8 %copy-start.15 = (f32[2064]{0:T(1024)S(1)}, f32[2064]{0:T(1024)}, u32[]{:S(2)}) copy-start(f32[2064]{0:T(1024)} %get-tuple-element.151) | copy-start | bytes 24772
  285.8 6.8 %copy-start.16 = (f32[2064]{0:T(1024)S(1)}, f32[2064]{0:T(1024)}, u32[]{:S(2)}) copy-start(f32[2064]{0:T(1024)} %get-tuple-element.152) | copy-start | bytes 24772
  285.8 6.8 %copy-start.17 = (f32[2064]{0:T(1024)S(1)}, f32[2064]{0:T(1024)}, u32[]{:S(2)}) copy-start(f32[2064]{0:T(1024)} %get-tuple-element.153) | copy-start | bytes 24772
  285.9 6.8 %copy-start.18 = (f32[2064]{0:T(1024)S(1)}, f32[2064]{0:T(1024)}, u32[]{:S(2)}) copy-start(f32[2064]{0:T(1024)} %get-tuple-element.154) | copy-start | bytes 24772
  285.9 6.8 %copy-start.19 = (f32[2064]{0:T(1024)S(1)}, f32[2064]{0:T(1024)}, u32[]{:S(2)}) copy-start(f32[2064]{0:T(1024)} %get-tuple-element.155) | copy-start | bytes 24772
  285.9 6.8 %copy-start.20 = (f32[2064]{0:T(1024)S(1)}, f32[2064]{0:T(1024)}, u32[]{:S(2)}) copy-start(f32[2064]{0:T(1024)} %get-tuple-element.156) | copy-start | bytes 24772
  285.9 6.8 %copy-start.21 = (f32[2064]{0:T(1024)S(1)}, f32[2064]{0:T(1024)}, u32[]{:S(2)}) copy-start(f32[2064]{0:T(1024)} %get-tuple-element.157) | copy-start | bytes 24772
  285.9 6.8 %copy-start.22 = (f32[2064]{0:T(1024)S(1)}, f32[2064]{0:T(1024)}, u32[]{:S(2)}) copy-start(f32[2064]{0:T(1024)} %get-tuple-element.158) | copy-start | bytes 24772
  285.9 6.8 %copy-start.23 = (f32[2064]{0:T(1024)S(1)}, f32[2064]{0:T(1024)}, u32[]{:S(2)}) copy-start(f32[2064]{0:T(1024)} %get-tuple-element.159) | copy-start | bytes 24772
  285.9 6.8 %copy-start.24 = (f32[2064]{0:T(1024)S(1)}, f32[2064]{0:T(1024)}, u32[]{:S(2)}) copy-start(f32[2064]{0:T(1024)} %get-tuple-element.160) | copy-start | bytes 24772
  285.9 6.8 %copy-start.25 = (f32[2064]{0:T(1024)S(1)}, f32[2064]{0:T(1024)}, u32[]{:S(2)}) copy-start(f32[2064]{0:T(1024)} %get-tuple-element.161) | copy-start | bytes 24772
  285.9 6.8 %copy-start.26 = (f32[2064]{0:T(1024)S(1)}, f32[2064]{0:T(1024)}, u32[]{:S(2)}) copy-start(f32[2064]{0:T(1024)} %get-tuple-element.162) | copy-start | bytes 24772
  285.9 6.8 %copy-start.27 = (f32[2064]{0:T(1024)S(1)}, f32[2064]{0:T(1024)}, u32[]{:S(2)}) copy-start(f32[2064]{0:T(1024)} %get-tuple-element.163) | copy-start | bytes 24772
  286.0 6.8 %copy-start.28 = (f32[2064]{0:T(1024)S(1)}, f32[2064]{0:T(1024)}, u32[]{:S(2)}) copy-start(f32[2064]{0:T(1024)} %get-tuple-element.164) | copy-start | bytes 24772
  286.0 6.8 %copy-start.29 = (f32[2064]{0:T(1024)S(1)}, f32[2064]{0:T(1024)}, u32[]{:S(2)}) copy-start(f32[2064]{0:T(1024)} %get-tuple-element.165) | copy-start | bytes 24772
  286.0 6.8 %copy-start.30 = (f32[2064]{0:T(1024)S(1)}, f32[2064]{0:T(1024)}, u32[]{:S(2)}) copy-start(f32[2064]{0:T(1024)} %get-tuple-element.166) | copy-start | bytes 24772
  286.0 6.8 %copy-start.31 = (f32[2064]{0:T(1024)S(1)}, f32[2064]{0:T(1024)}, u32[]{:S(2)}) copy-start(f32[2064]{0:T(1024)} %get-tuple-element.167) | copy-start | bytes 24772
  292.8 13.0 %copy-start.10 = (f32[2064]{0:T(1024)S(1)}, f32[2064]{0:T(1024)}, u32[]{:S(2)}) copy-start(f32[2064]{0:T(1024)} %get-tuple-element.147) | copy-start | bytes 24772
  292.8 13.0 %copy-start.11 = (f32[2064]{0:T(1024)S(1)}, f32[2064]{0:T(1024)}, u32[]{:S(2)}) copy-start(f32[2064]{0:T(1024)} %get-tuple-element.148) | copy-start | bytes 24772
  292.8 13.0 %copy-start.12 = (f32[2064]{0:T(1024)S(1)}, f32[2064]{0:T(1024)}, u32[]{:S(2)}) copy-start(f32[2064]{0:T(1024)} %get-tuple-element.149) | copy-start | bytes 24772
  292.8 13.0 %copy-start.13 = (f32[2064]{0:T(1024)S(1)}, f32[2064]{0:T(1024)}, u32[]{:S(2)}) copy-start(f32[2064]{0:T(1024)} %get-tuple-element.150) | copy-start | bytes 24772
  305.8 5.6 %copy-start.6 = (bf16[256,344]{0,1:T(8,128)(2,1)S(1)}, bf16[256,344]{0,1:T(8,128)(2,1)}, u32[]{:S(2)}) copy-start(bf16[256,344]{0,1:T(8,128)(2,1)} %copy-done.5) | copy-start | bytes 528388
  343.7 111.9 %copy-start.1 = (bf16[1,344,2064]{2,1,0:T(8,128)(2,1)S(1)}, bf16[1,344,2064]{2,1,0:T(8,128)(2,1)}, u32[]{:S(2)}) copy-start(bf16[1,344,2064]{2,1,0:T(8,128)(2,1)} %param.21) | copy-start | bytes 4260100
  (7 other events, 13.5 us)
Sparse Core Ops, SparseCore 0:
  61.7 101.3 all-gather.4
  168.5 100.4 all-gather.6
  343.8 106.4 all-reduce.59
